TPU v7x, 32 devices: a whole 2x2x4 slice. The times are simulated.
32 devices in a mesh: row: 4 (over y, core), col: 8 (over z, x).
Axes of the slice: x: 2, y: 2, z: 4, core: 2. Of those that a mesh axis runs over, the one named last changes fastest.
Arguments:
- positions: float32 [3, 512], P(None, ('row', 'col')), as said below
- thermal_noise: float32 [32, 3, 512], P(None, None, ('row', 'col')), as said below
Outputs:
- displacement: float32 [32, 3, 512], P(None, None, ('row', 'col'))
Inputs may be any that keep to these rules, and one draw needn't show every extreme that they name: `positions`: any two particles are at least 1.0 apart. `thermal_noise`: finite real entries.
All inputs are finite; a program needn't handle non-finite values.
Results may differ from a plain program's by a relative error of at most 0.0013.
Values may be sent and summed in bfloat16 or wider, within the bound.
A program may use at most 64 MiB of HBM per device.

v0:
```python
import jax
import jax.numpy as jnp
from jax import lax
from jax.sharding import PartitionSpec as P


def pair_tensor(rows_pos, cols_pos, retain):
    offsets = [rows_pos[a][None, :] - cols_pos[a][:, None] for a in range(3)]
    squared = offsets[0] * offsets[0] + offsets[1] * offsets[1] + offsets[2] * offsets[2]
    guarded = jnp.where(retain, squared, 4.0)
    inverse = lax.rsqrt(guarded)
    distance = guarded * inverse
    correlation = distance < 2.0
    inverse_cube = inverse * inverse * inverse
    inverse_fifth = inverse_cube * inverse * inverse
    isotropic = jnp.where(
        correlation, 1.0 - 0.28125 * distance, 0.75 * inverse + 0.5 * inverse_cube
    )
    dyadic = jnp.where(correlation, 0.09375 * inverse, 0.75 * inverse_cube - 1.5 * inverse_fifth)
    isotropic = jnp.where(retain, isotropic, 0.0)
    dyadic = jnp.where(retain, dyadic, 0.0)
    columns = []
    for b in range(3):
        elements = []
        for a in range(3):
            element = dyadic * offsets[a] * offsets[b]
            if a == b:
                element = element + isotropic
            elements.append(element)
        columns.append(jnp.stack(elements, axis=1))
    return jnp.stack(columns, axis=0)


def half_image(pos_rows, pos_cols, vec_rows, vec_cols, own_vector):
    row_devices = lax.axis_size("row")
    col_devices = lax.axis_size("col")
    row_index = lax.axis_index("row")
    col_index = lax.axis_index("col")
    samples = own_vector.shape[0]
    per_device = own_vector.shape[2]
    row_count = pos_rows.shape[1]
    row_label = row_index * col_devices * per_device + lax.iota(jnp.int32, row_count)
    group_size = min(row_devices, max(1, 128 // per_device))
    width = group_size * per_device
    group_count = row_devices // group_size
    sum_rows = jnp.zeros((samples, 3, row_count), jnp.float32)
    sum_cols = jnp.zeros((samples, 3, per_device * row_devices), jnp.float32)

    def add_group(group, totals):
        sum_rows, sum_cols = totals
        start = group * width
        cols_pos = lax.dynamic_slice_in_dim(pos_cols, start, width, 1)
        cols_vec = lax.dynamic_slice_in_dim(vec_cols, start, width, 2)
        local_cols = lax.iota(jnp.int32, width)
        segment = group * group_size + local_cols // per_device
        col_label = (segment * col_devices + col_index) * per_device + local_cols % per_device
        keep = segment >= row_index
        upper = (segment != row_index)[:, None] | (row_label[None, :] < col_label[:, None])
        retain = keep[:, None] & upper & (row_label[None, :] != col_label[:, None])
        tensor = pair_tensor(pos_rows, cols_pos, retain).astype(jnp.bfloat16)
        sum_rows = sum_rows + jnp.einsum(
            "kbj,bjai->kai", cols_vec, tensor, preferred_element_type=jnp.float32
        )
        credit = jnp.einsum("kai,bjai->kbj", vec_rows, tensor, preferred_element_type=jnp.float32)
        previous = lax.dynamic_slice_in_dim(sum_cols, start, width, 2)
        sum_cols = lax.dynamic_update_slice_in_dim(sum_cols, previous + credit, start, 2)
        return (sum_rows, sum_cols)

    totals = (sum_rows, sum_cols)
    totals = lax.fori_loop(row_index // group_size, group_count, add_group, totals)
    sum_rows, sum_cols = totals
    mobility_image = own_vector + lax.psum_scatter(sum_rows, "col", scatter_dimension=2, tiled=True)
    return mobility_image + lax.psum_scatter(sum_cols, "row", scatter_dimension=2, tiled=True)


def on_device(positions, thermal_noise):
    squares = lax.psum(jnp.sum(thermal_noise * thermal_noise, axis=(1, 2)), ("row", "col"))
    noise_length = jnp.sqrt(squares + 1e-06)
    basis_one = thermal_noise / noise_length[:, None, None]
    pos_cols, cols_one = (
        lax.all_gather(positions, "row", axis=1, tiled=True),
        lax.all_gather(basis_one, "row", axis=2, tiled=True),
    )
    pos_rows, rows_wide = (
        lax.all_gather(positions, "col", axis=1, tiled=True),
        lax.all_gather(basis_one, "col", axis=2, tiled=True),
    )
    image_one = half_image(
        pos_rows, pos_cols, rows_wide.astype(jnp.bfloat16), cols_one.astype(jnp.bfloat16), basis_one
    )
    alpha_one = lax.psum(jnp.sum(basis_one * image_one, axis=(1, 2)), ("row", "col"))
    remainder = image_one - alpha_one[:, None, None] * basis_one
    beta_squared = lax.psum(jnp.sum(remainder * remainder, axis=(1, 2)), ("row", "col"))
    beta_one = jnp.sqrt(beta_squared + 1e-06)
    basis_two = remainder / beta_one[:, None, None]
    narrow_two = basis_two.astype(jnp.bfloat16)
    cols_two = lax.all_gather(narrow_two, "row", axis=2, tiled=True)
    rows_two = lax.all_gather(narrow_two, "col", axis=2, tiled=True)
    image_two = half_image(pos_rows, pos_cols, rows_two, cols_two, basis_two)
    alpha_two = lax.psum(jnp.sum(basis_two * image_two, axis=(1, 2)), ("row", "col"))
    det_root = jnp.sqrt(alpha_one * alpha_two - beta_one * beta_one)
    trace_root = jnp.sqrt(alpha_one + alpha_two + 2.0 * det_root)
    weight_one = (alpha_one + det_root) / trace_root
    weight_two = beta_one / trace_root
    return (
        0.5
        * noise_length[:, None, None]
        * (weight_one[:, None, None] * basis_one + weight_two[:, None, None] * basis_two)
    )


def solution(mesh):
    return jax.shard_map(
        on_device,
        mesh=mesh,
        in_specs=(P(None, ("row", "col")), P(None, None, ("row", "col"))),
        out_specs=P(None, None, ("row", "col")),
        check_vma=False,
    )
```

profile of v0, /device:TPU:0, one launch (start us, length us, event | category | flops | bytes accessed | tf_op | source)
XLA Modules:
  0.0 451.7 jit_solution(3374881495807771110)
XLA Ops:
  6.5 0.0 reduce-scatter.7.cloned.1.call-start
  6.5 0.0 copy-start.3
  6.5 0.7 copy-done.3
  7.2 0.0 copy-start
  7.2 28.1 %all-gather = f32[8,16,3]{1,2,0:T(4,128)S(1)} all-gather(f32[1,16,3]{1,2,0:T(4,128)S(1)} %bitcast.133), channel_id=1, replica_groups=mesh['row'=4,'col'=8] {'col'}, dimensions={0}, use_global_device_ids=true | all-gather | bytes 1728 | tf_op jit(solution)/shard_map/all_gather | solution.py:85
  35.3 5.2 %all-gather.1 = f32[4,16,3]{1,2,0:T(4,128)S(1)} all-gather(f32[1,16,3]{1,2,0:T(4,128)S(1)} %bitcast.134), channel_id=1, replica_groups=mesh['row'=4,'col'=8] {'row'}, dimensions={0}, use_global_device_ids=true | all-gather | bytes 960 | tf_op jit(solution)/shard_map/all_gather | solution.py:81
  40.5 0.0 copy-done
  40.5 38.9 %psum.28 = f32[32]{0:T(128)S(1)} all-reduce(f32[32]{0:T(128)S(1)} %multiply_reduce_fusion.3), channel_id=1, replica_groups=mesh['row'=4,'col'=8] {'row','col'}, use_global_device_ids=true, to_apply=%region_1.0 | all-reduce | flops 32 | bytes 256 | tf_op jit(solution)/shard_map/psum | solution.py:77
  79.5 5.5 %all_gather.20 = bf16[32,3,64]{0,2,1:T(8,128)(2,1)S(1)} all-gather(bf16[32,3,16]{0,2,1:T(8,128)(2,1)S(1)} %convert.110), channel_id=1, replica_groups=mesh['row'=4,'col'=8] {'row'}, dimensions={2}, use_global_device_ids=true | all-gather | bytes 15360 | tf_op jit(solution)/shard_map/all_gather | solution.py:82
  85.0 0.1 copy.39
  85.1 30.6 %all_gather.21 = bf16[32,3,128]{0,2,1:T(8,128)(2,1)S(1)} all-gather(bf16[32,3,16]{0,2,1:T(8,128)(2,1)S(1)} %get-tuple-element.415), channel_id=1, replica_groups=mesh['row'=4,'col'=8] {'col'}, dimensions={2}, use_global_device_ids=true | all-gather | bytes 27648 | tf_op jit(solution)/shard_map/all_gather | solution.py:86
  115.6 0.1 copy.40
  115.7 0.1 reshape.5452
  115.8 0.1 reshape.5454
  115.9 0.7 while.30
  116.0 0.2 fusion.88
  116.3 0.2 fusion.90
  116.4 0.2 fusion.89
  116.6 0.7 copy.42
  117.4 0.0 reduce-scatter.7.cloned.1.call-update
  117.4 0.0 reduce-scatter.5.cloned.1.call-start
  117.5 0.8 copy.41
  118.3 0.0 reduce-scatter.5.cloned.1.call-update
  118.3 0.0 reduce-scatter.11.cloned.1.call-start
  118.3 17.6 %reduce-scatter.7.cloned.1.call-done = f32[32,3,16]{0,2,1:T(8,128)} async-done(((f32[32,3,64]{0,2,1:T(8,128)}), f32[32,3,16]{0,2,1:T(8,128)}) %reduce-scatter.7.cloned.1.call-update) | async-done | bytes 6160 | tf_op jit(solution)/shard_map/reduce_scatter | solution.py:73
  135.9 0.0 copy-start.1
  135.9 65.3 %reduce-scatter.5.cloned.1.call-done = f32[32,3,16]{0,2,1:T(8,128)} async-done(((f32[32,3,128]{0,2,1:T(8,128)}), f32[32,3,16]{0,2,1:T(8,128)}) %reduce-scatter.5.cloned.1.call-update) | async-done | bytes 6160 | tf_op jit(solution)/shard_map/reduce_scatter | solution.py:72
  201.2 0.0 copy-start.2
  201.2 0.8 multiply_reduce_fusion.2
  202.1 40.1 %psum.29 = f32[32]{0:T(128)S(1)} all-reduce(f32[32]{0:T(128)S(1)} %multiply_reduce_fusion.2), channel_id=1, replica_groups=mesh['row'=4,'col'=8] {'row','col'}, use_global_device_ids=true, to_apply=%region_7.8 | all-reduce | flops 32 | bytes 256 | tf_op jit(solution)/shard_map/psum | solution.py:91
  242.2 0.0 copy-done.1
  242.2 0.0 copy-done.2
  242.2 39.1 %psum.30 = f32[32]{0:T(128)S(1)} all-reduce(f32[32]{0:T(128)S(1)} %get-tuple-element.413), channel_id=1, replica_groups=mesh['row'=4,'col'=8] {'row','col'}, use_global_device_ids=true, to_apply=%region_9.10 | all-reduce | flops 32 | bytes 256 | tf_op jit(solution)/shard_map/psum | solution.py:93
  281.3 30.5 %all_gather.23 = bf16[32,3,128]{0,2,1:T(8,128)(2,1)S(1)} all-gather(bf16[32,3,16]{0,2,1:T(8,128)(2,1)S(1)} %fusion.71), channel_id=1, replica_groups=mesh['row'=4,'col'=8] {'col'}, dimensions={2}, use_global_device_ids=true | all-gather | bytes 27648 | tf_op jit(solution)/shard_map/all_gather | solution.py:98
  311.9 5.5 %all_gather.22 = bf16[32,3,64]{0,2,1:T(8,128)(2,1)S(1)} all-gather(bf16[32,3,16]{0,2,1:T(8,128)(2,1)S(1)} %fusion.71), channel_id=1, replica_groups=mesh['row'=4,'col'=8] {'row'}, dimensions={2}, use_global_device_ids=true | all-gather | bytes 15360 | tf_op jit(solution)/shard_map/all_gather | solution.py:97
  317.4 0.1 copy.44
  317.5 0.1 copy.43
  317.6 0.7 while.31
  317.7 0.2 fusion.94
  318.0 0.2 fusion.96
  318.2 0.2 fusion.95
  318.4 0.7 copy.46
  319.1 0.0 reduce-scatter.11.cloned.1.call-update
  319.1 0.0 reduce-scatter.9.cloned.1.call-start
  319.2 0.8 copy.45
  320.0 0.0 reduce-scatter.9.cloned.1.call-update
  320.0 18.4 %reduce-scatter.11.cloned.1.call-done = f32[32,3,16]{0,2,1:T(8,128)} async-done(((f32[32,3,64]{0,2,1:T(8,128)}), f32[32,3,16]{0,2,1:T(8,128)}) %reduce-scatter.11.cloned.1.call-update) | async-done | bytes 6160 | tf_op jit(solution)/shard_map/reduce_scatter | solution.py:73
  338.4 65.2 %reduce-scatter.9.cloned.1.call-done = f32[32,3,16]{0,2,1:T(8,128)} async-done(((f32[32,3,128]{0,2,1:T(8,128)}), f32[32,3,16]{0,2,1:T(8,128)}) %reduce-scatter.9.cloned.1.call-update) | async-done | bytes 6160 | tf_op jit(solution)/shard_map/reduce_scatter | solution.py:72
  403.6 0.8 multiply_reduce_fusion
  404.4 40.2 %psum.31 = f32[32]{0:T(128)S(1)} all-reduce(f32[32]{0:T(128)S(1)} %multiply_reduce_fusion), channel_id=1, replica_groups=mesh['row'=4,'col'=8] {'row','col'}, use_global_device_ids=true, to_apply=%region_15.16 | all-reduce | flops 32 | bytes 256 | tf_op jit(solution)/shard_map/psum | solution.py:100
  444.6 0.6 add_multiply_fusion
  (30 shorter events, 0.3 us)
Async XLA Ops:
  6.5 129.4 %reduce-scatter.7.cloned.1.call-start = ((), (), s32[]{:S(2)}) async-start(), calls=%async_computation.5 | async-start | bytes 122880 | tf_op jit(solution)/shard_map/reduce_scatter | solution.py:73
  6.5 0.7 copy-start.3
  7.2 33.2 %copy-start = (f32[32,3,16]{0,2,1:T(8,128)S(1)}, f32[32,3,16]{0,2,1:T(8,128)}, u32[]{:S(2)}) copy-start(f32[32,3,16]{0,2,1:T(8,128)} %param.7) | copy-start | bytes 18436
  117.4 83.8 %reduce-scatter.5.cloned.1.call-start = ((), (), s32[]{:S(2)}) async-start(), calls=%async_computation.4 | async-start | bytes 221184 | tf_op jit(solution)/shard_map/reduce_scatter | solution.py:72
  118.3 220.2 %reduce-scatter.11.cloned.1.call-start = ((), (), s32[]{:S(2)}) async-start(), calls=%async_computation.7 | async-start | bytes 122880 | tf_op jit(solution)/shard_map/reduce_scatter | solution.py:73
  135.9 106.2 %copy-start.1 = (f32[32,3,16]{0,2,1:T(8,128)S(1)}, f32[32,3,16]{0,2,1:T(8,128)}, u32[]{:S(2)}) copy-start(f32[32,3,16]{0,2,1:T(8,128)} %reduce-scatter.7.cloned.1.call-done) | copy-start | bytes 18436
  201.2 40.9 %copy-start.2 = (f32[32,3,16]{0,2,1:T(8,128)S(1)}, f32[32,3,16]{0,2,1:T(8,128)}, u32[]{:S(2)}) copy-start(f32[32,3,16]{0,2,1:T(8,128)} %reduce-scatter.5.cloned.1.call-done) | copy-start | bytes 18436
  319.1 84.5 %reduce-scatter.9.cloned.1.call-start = ((), (), s32[]{:S(2)}) async-start(), calls=%async_computation.6 | async-start | bytes 221184 | tf_op jit(solution)/shard_map/reduce_scatter | solution.py:72
Sparse Core Ops, SparseCore 0:
  117.5 18.3 reduce-scatter.6
  139.2 61.9 reduce-scatter.4
  319.2 19.1 reduce-scatter.10
  341.6 61.9 reduce-scatter.8
where the time goes:
time: 453 us; the launch traced here: 452 us
  blocking collectives  264 us (58%)
  waiting for transfers between devices  167 us (37%)
  between operations  13.2 us (3%)
    reduce_scatter x2, waiting for transfers between devices, half_image(): lax.psum_scatter(sum_rows, 'col', scatter_dimension=2, tiled=True)  130 us
    psum x1, blocking collectives, on_device(): lax.psum(jnp.sum(basis_two * image_two, axis=(1, 2)), ('row', 'col'))  40.2 us
    psum x1, blocking collectives, on_device(): lax.psum(jnp.sum(basis_one * image_one, axis=(1, 2)), ('row', 'col'))  40.1 us
    psum x1, blocking collectives, on_device(): lax.psum(jnp.sum(remainder * remainder, axis=(1, 2)), ('row', 'col'))  39.1 us
    psum x1, blocking collectives, on_device(): lax.psum(jnp.sum(thermal_noise * thermal_noise, axis=(1, 2)), ('row', 'co...  38.9 us
    reduce_scatter x2, waiting for transfers between devices, half_image(): lax.psum_scatter(sum_cols, 'row', scatter_dimension=2, tiled=True)  36 us
    all_gather x1, blocking collectives, on_device(): lax.all_gather(basis_one, 'col', axis=2, tiled=True)  30.6 us
    all_gather x1, blocking collectives, on_device(): rows_two = lax.all_gather(narrow_two, 'col', axis=2, tiled=True)  30.5 us
  transfers between devices with their start and end apart: 4, of which 4 were waited for; matrix products, arithmetic and copies ran while one was open for 0% of the time, Pallas kernels for 0%

commit v1 on v0

--- a/solution.py
+++ b/solution.py
@@ -83,7 +83,7 @@
     )
     pos_rows, rows_wide = (
         lax.all_gather(positions, "col", axis=1, tiled=True),
-        lax.all_gather(basis_one, "col", axis=2, tiled=True),
+        jnp.concatenate(lax.all_gather(basis_one, "col"), axis=2),
     )
     image_one = half_image(
         pos_rows, pos_cols, rows_wide.astype(jnp.bfloat16), cols_one.astype(jnp.bfloat16), basis_one

time: 453 us -> 371 us (0.82)
  waiting for transfers between devices: 167 us -> 0 us
  blocking collectives: 264 us -> 360 us
  between operations: 13.2 us -> 1.5 us
    reduce_scatter x4 -> x0, waiting for transfers between devices: 166 us -> none  [the longest x2 130 us: half_image(): lax.psum_scatter(sum_rows, 'col', scatter_dimension=2, tiled=True)]
    unnamed x0 -> x4, blocking collectives: none -> 99.9 us
  transfers between devices with their start and end apart: 4 -> 0, of which waited for: 4 -> 0; matrix products, arithmetic and copies ran while one was open for 0% -> 0% of each run, Pallas kernels for 0% -> 0%
where the time goes in v1:
time: 371 us; the launch traced here: 369 us
  blocking collectives  360 us (97%)
  local copies, waits for them, and re-layouts  4.69 us (1%)
    unnamed x4, blocking collectives  99.9 us
    psum x1, blocking collectives, on_device(): lax.psum(jnp.sum(thermal_noise * thermal_noise, axis=(1, 2)), ('row', 'co...  42 us
    psum x1, blocking collectives, on_device(): lax.psum(jnp.sum(remainder * remainder, axis=(1, 2)), ('row', 'col'))  41 us
    psum x1, blocking collectives, on_device(): lax.psum(jnp.sum(basis_two * image_two, axis=(1, 2)), ('row', 'col'))  37 us
    psum x1, blocking collectives, on_device(): lax.psum(jnp.sum(basis_one * image_one, axis=(1, 2)), ('row', 'col'))  36.8 us
    all_gather x1, blocking collectives, on_device(): lax.all_gather(basis_one, 'col')  30.8 us
    all_gather x1, blocking collectives, on_device(): rows_two = lax.all_gather(narrow_two, 'col', axis=2, tiled=True)  30.6 us
    all_gather x1, blocking collectives, on_device(): lax.all_gather(positions, 'col', axis=1, tiled=True)  26.1 us

profile of v1, /device:TPU:0, one launch (start us, length us, event | category | flops | bytes accessed | tf_op | source)
XLA Modules:
  0.0 368.9 jit_solution(11774549185331810694)
XLA Ops:
  0.0 0.0 copy-start
  0.0 0.7 copy-done
  0.8 42.0 %psum.28 = f32[32]{0:T(128)S(1)} all-reduce(f32[32]{0:T(128)S(1)} %multiply_reduce_fusion.2), channel_id=1, replica_groups=mesh['row'=4,'col'=8] {'row','col'}, use_global_device_ids=true, to_apply=%region_1.0 | all-reduce | flops 32 | bytes 256 | tf_op jit(solution)/shard_map/psum | solution.py:77
  42.8 0.1 copy.57
  42.9 30.8 %all-gather = bf16[256,3,16]{2,1,0:T(4,128)(2,1)S(1)} all-gather(bf16[32,3,16]{2,1,0:T(4,128)(2,1)S(1)} %copy.57), channel_id=2, replica_groups=mesh['row'=4,'col'=8] {'col'}, dimensions={0}, use_global_device_ids=true | all-gather | bytes 27648 | tf_op jit(solution)/shard_map/all_gather | solution.py:86
  73.7 0.2 copy.58
  73.9 0.1 copy.60
  74.0 5.5 %all_gather.23 = bf16[32,3,64]{0,2,1:T(8,128)(2,1)S(1)} all-gather(bf16[32,3,16]{0,2,1:T(8,128)(2,1)S(1)} %get-tuple-element.435), channel_id=1, replica_groups=mesh['row'=4,'col'=8] {'row'}, dimensions={2}, use_global_device_ids=true | all-gather | bytes 15360 | tf_op jit(solution)/shard_map/all_gather | solution.py:82
  79.5 0.0 copy-start.1
  79.5 0.1 copy.59
  79.6 0.6 copy-done.1
  80.2 26.1 %all-gather.1 = f32[8,16,3]{1,2,0:T(4,128)S(1)} all-gather(f32[1,16,3]{1,2,0:T(4,128)S(1)} %bitcast.141), channel_id=1, replica_groups=mesh['row'=4,'col'=8] {'col'}, dimensions={0}, use_global_device_ids=true | all-gather | bytes 1728 | tf_op jit(solution)/shard_map/all_gather | solution.py:85
  106.3 0.1 reshape.5457
  106.4 5.2 %all-gather.2 = f32[4,16,3]{1,2,0:T(4,128)S(1)} all-gather(f32[1,16,3]{1,2,0:T(4,128)S(1)} %bitcast.142), channel_id=1, replica_groups=mesh['row'=4,'col'=8] {'row'}, dimensions={0}, use_global_device_ids=true | all-gather | bytes 960 | tf_op jit(solution)/shard_map/all_gather | solution.py:81
  111.6 0.1 reshape.5459
  111.7 0.7 while.30
  111.8 0.2 fusion.90
  112.0 0.2 fusion.92
  112.2 0.2 fusion.91
  112.4 0.2 copy.61
  112.6 38.0 %all-reduce = f32[32,3,128]{0,1,2:T(4,128)S(1)} all-reduce(f32[32,3,128]{0,1,2:T(4,128)S(1)} %copy.61), channel_id=3, replica_groups=mesh['row'=4,'col'=8] {'col'}, use_global_device_ids=true, to_apply=%region_4.5.clone | all-reduce | flops 12288 | bytes 98304
  150.6 0.0 copy-start.3
  150.6 0.6 copy-done.3
  151.3 0.6 dynamic-slice
  152.6 0.1 copy.63
  152.7 0.0 copy-start.2
  152.7 11.7 %all-reduce.1 = f32[32,3,64]{0,1,2:T(4,128)S(1)} all-reduce(f32[32,3,64]{0,1,2:T(4,128)S(1)} %copy.63), channel_id=4, replica_groups=mesh['row'=4,'col'=8] {'row'}, use_global_device_ids=true, to_apply=%region_5.6.clone | all-reduce | flops 6144 | bytes 49152
  164.4 0.0 copy-done.2
  164.4 0.7 dynamic-slice.2
  165.8 36.8 %psum.29 = f32[32]{0:T(128)S(1)} all-reduce(f32[32]{0:T(128)S(1)} %get-tuple-element.433), channel_id=1, replica_groups=mesh['row'=4,'col'=8] {'row','col'}, use_global_device_ids=true, to_apply=%region_7.8 | all-reduce | flops 32 | bytes 256 | tf_op jit(solution)/shard_map/psum | solution.py:91
  202.6 41.0 %psum.30 = f32[32]{0:T(128)S(1)} all-reduce(f32[32]{0:T(128)S(1)} %multiply_reduce_fusion), channel_id=1, replica_groups=mesh['row'=4,'col'=8] {'row','col'}, use_global_device_ids=true, to_apply=%region_9.10 | all-reduce | flops 32 | bytes 256 | tf_op jit(solution)/shard_map/psum | solution.py:93
  243.6 30.6 %all_gather.27 = bf16[32,3,128]{0,2,1:T(8,128)(2,1)S(1)} all-gather(bf16[32,3,16]{0,2,1:T(8,128)(2,1)S(1)} %fusion.73), channel_id=1, replica_groups=mesh['row'=4,'col'=8] {'col'}, dimensions={2}, use_global_device_ids=true | all-gather | bytes 27648 | tf_op jit(solution)/shard_map/all_gather | solution.py:98
  274.2 0.1 copy.66
  274.3 5.5 %all_gather.26 = bf16[32,3,64]{0,2,1:T(8,128)(2,1)S(1)} all-gather(bf16[32,3,16]{0,2,1:T(8,128)(2,1)S(1)} %fusion.73), channel_id=1, replica_groups=mesh['row'=4,'col'=8] {'row'}, dimensions={2}, use_global_device_ids=true | all-gather | bytes 15360 | tf_op jit(solution)/shard_map/all_gather | solution.py:97
  279.8 0.1 copy.65
  279.9 0.7 while.31
  280.0 0.2 fusion.96
  280.3 0.2 fusion.98
  280.5 0.2 fusion.97
  280.7 0.2 copy.67
  280.8 38.7 %all-reduce.2 = f32[32,3,128]{0,1,2:T(4,128)S(1)} all-reduce(f32[32,3,128]{0,1,2:T(4,128)S(1)} %copy.67), channel_id=5, replica_groups=mesh['row'=4,'col'=8] {'col'}, use_global_device_ids=true, to_apply=%region_12.13.clone | all-reduce | flops 12288 | bytes 98304
  319.5 0.1 copy.69
  319.6 11.5 %all-reduce.3 = f32[32,3,64]{0,1,2:T(4,128)S(1)} all-reduce(f32[32,3,64]{0,1,2:T(4,128)S(1)} %copy.69), channel_id=6, replica_groups=mesh['row'=4,'col'=8] {'row'}, use_global_device_ids=true, to_apply=%region_13.14.clone | all-reduce | flops 6144 | bytes 49152
  331.2 37.0 %psum.31 = f32[32]{0:T(128)S(1)} all-reduce(f32[32]{0:T(128)S(1)} %fusion.71), channel_id=1, replica_groups=mesh['row'=4,'col'=8] {'row','col'}, use_global_device_ids=true, to_apply=%region_15.16 | all-reduce | flops 32 | bytes 256 | tf_op jit(solution)/shard_map/psum | solution.py:100
  368.2 0.6 add_multiply_fusion
  (35 shorter events, 0.4 us)
Async XLA Ops:
  0.0 0.7 copy-start
  79.5 0.7 copy-start.1
  150.6 0.7 copy-start.3
  152.7 11.7 %copy-start.2 = (u32[32]{0:T(128)S(1)}, u32[32]{0:T(128)}, u32[]{:S(2)}) copy-start(u32[32]{0:T(128)} %constant.271) | copy-start | bytes 388
